TPU v7x, 32 devices: a whole 2x2x4 slice. The times are simulated.
32 devices in a mesh: grp: 4 (over y, x), mem: 8 (over z, core).
Axes of the slice: x: 2, y: 2, z: 4, core: 2. Of those that a mesh axis runs over, the one named last changes fastest.
Arguments:
- factors: bfloat16 [32, 512, 2048], P(('grp', 'mem')), may hold values from -1 to 1
- occ_energy: bfloat16 [32], P(('grp', 'mem')), may hold values from -1.5 to -0.29882812
- vir_energy: bfloat16 [512], replicated, may hold values from 0.3984375 to 3
- pair_code: int32 [4, 8, 3], P('grp'), may hold values from 0 to 2
- pair_count: int32 [4, 8], P('grp'), may hold values from 1 to 3
Outputs:
- aux_density: bfloat16 [32, 512, 2048], P(('grp', 'mem'))
- lagrangian: bfloat16 [32, 512, 2048], P(('grp', 'mem'))
Inputs may be any that keep to these rules, and one draw needn't show every extreme that they name: `pair_code`: only the first pair_count entries of a device's list are read; entries may repeat.
All inputs are finite; a program needn't handle non-finite values.
Results may differ from a plain program's by a relative error of at most 0.0056.
Values may be sent and summed in bfloat16 or wider, within the bound.
No kernel may reach another device: no remote copies, remote signals or barrier semaphores. Data moves between devices by JAX's collectives and lax.ppermute only.
A program may use at most 128 MiB of HBM per device.

v0:
```python
import jax
import jax.numpy as jnp
from jax import lax
from jax.sharding import PartitionSpec as P

OCC_DEV = 1
ROUNDS = 2


def partner(value, axis, distance):
    mask = 2**distance
    pairs = [(source, source ^ mask) for source in range(lax.axis_size(axis))]
    return lax.ppermute(value, axis, pairs)


def decode_pair(code):
    round_no = code // (OCC_DEV * OCC_DEV)
    left_orb = code // OCC_DEV % OCC_DEV
    right_orb = code % OCC_DEV
    return (round_no, left_orb, right_orb)


def add_at(target, indices, contribution):
    zero_index = jnp.zeros((), jnp.int32)
    anchor = tuple(indices) + (zero_index,) * contribution.ndim
    extent = (1,) * len(indices) + contribution.shape
    current = lax.dynamic_slice(target, anchor, extent)
    return lax.dynamic_update_slice(target, current + contribution.reshape(extent), anchor)


def outer_terms(amp_tile):
    return lax.dot_general(
        amp_tile, amp_tile, (((1,), (1,)), ((), ())), preferred_element_type=jnp.float32
    )


def near_product(amp_tile, right_block):
    return jnp.dot(amp_tile, right_block, preferred_element_type=jnp.float32)


def far_product(amp_tile, left_block):
    return lax.dot_general(
        amp_tile, left_block, (((0,), (0,)), ((), ())), preferred_element_type=jnp.float32
    )


def per_device(factors, occ_energy, vir_energy, pair_code, pair_count):
    virtual = vir_energy.astype(jnp.float32)
    my_place = lax.axis_index("mem")
    group_codes = pair_code[0]
    group_counts = pair_count[0]
    my_codes = lax.dynamic_index_in_dim(group_codes, my_place, 0, keepdims=False)
    live_count = lax.dynamic_index_in_dim(group_counts, my_place, 0, keepdims=False)
    blocks_all = [factors]
    energy_list = [occ_energy]
    for round_idx in range(ROUNDS):
        visitor, visitor_energy = partner((factors, occ_energy), "mem", round_idx)
        blocks_all.append(visitor)
        energy_list.append(visitor_energy)
    stacked = jnp.stack(blocks_all)
    energy_all = jnp.stack(energy_list).astype(jnp.float32)
    vir_count = factors.shape[1]
    density_zero = jnp.zeros((vir_count, vir_count), jnp.float32)

    def pair_terms(slot_no):
        round_no, left_orb, right_orb = decode_pair(my_codes[slot_no])
        left_block = stacked[0, left_orb]
        right_block = stacked[round_no, right_orb]
        integrals = lax.dot_general(
            left_block, right_block, (((1,), (1,)), ((), ())), preferred_element_type=jnp.float32
        )
        denominator = (
            virtual[:, None]
            + virtual[None, :]
            - energy_all[0, left_orb]
            - energy_all[round_no, right_orb]
        )
        amp_tile = (integrals / denominator).astype(jnp.bfloat16)
        return (round_no, left_orb, right_orb, left_block, right_block, amp_tile)

    def pair_step(slot_no, carry_pair):
        density, totals = carry_pair
        round_no, left_orb, right_orb, left_block, right_block, amp_tile = pair_terms(slot_no)
        density = density + outer_terms(amp_tile)
        totals = add_at(
            totals, (jnp.zeros((), jnp.int32), left_orb), near_product(amp_tile, right_block)
        )
        totals = add_at(totals, (round_no, right_orb), far_product(amp_tile, left_block))
        return (density, totals)

    totals_zero = jnp.zeros((ROUNDS + 1,) + factors.shape, jnp.float32)
    density, totals = lax.fori_loop(0, live_count, pair_step, (density_zero, totals_zero))
    gathered = totals[0]
    for round_idx in range(ROUNDS):
        gathered = gathered + partner(totals[round_idx + 1], "mem", round_idx)
    density = lax.psum(density, "mem")
    density = lax.psum(density, "grp")
    density_scale = 1.0 / (8.0 * lax.axis_size("grp") * lax.axis_size("mem"))
    density_tile = (density * density_scale).astype(jnp.bfloat16)
    lagrangian = jnp.einsum(
        "ab,kbp->kap", density_tile, factors, preferred_element_type=jnp.float32
    )
    return (gathered.astype(jnp.bfloat16), lagrangian.astype(jnp.bfloat16))


def solution(mesh):
    in_specs = (
        P(("grp", "mem"), None, None),
        P(("grp", "mem")),
        P(),
        P("grp", None, None),
        P("grp", None),
    )
    out_specs = (P(("grp", "mem"), None, None), P(("grp", "mem"), None, None))
    return jax.shard_map(
        per_device, mesh=mesh, in_specs=in_specs, out_specs=out_specs, check_vma=False
    )
```

profile of v0, /device:TPU:0, one launch (start us, length us, event | category | flops | bytes accessed | tf_op | source)
XLA Modules:
  0.0 274.6 jit_solution(6055429350554140018)
XLA Ops:
  7.8 2.6 collective-permute-start.1
  11.9 1.2 constant_dynamic-slice_fusion.1
  13.4 43.7 %collective-permute-done.3 = bf16[1]{0:T(256)(128)(2,1)} collective-permute-done((bf16[1]{0:T(256)(128)(2,1)}, bf16[1]{0:T(256)(128)(2,1)}, u32[]{:S(2)}, u32[]{:S(2)}) %collective-permute-start.3) | collective-permute-done | bytes 34 | tf_op jit(solution)/shard_map/ppermute | solution.py:13
  57.1 1.3 maximum_convert_fusion
  58.3 5.5 %pad_maximum_fusion = bf16[3,1,512,2048]{3,2,1,0:T(8,128)(2,1)} fusion(bf16[1,1,512,2048]{3,2,1,0:T(8,128)(2,1)} %bitcast.11, bf16[1,1,512,2048]{3,2,1,0:T(8,128)(2,1)S(1)} %bitcast.93, bf16[1,1,512,2048]{3,2,1,0:T(8,128)(2,1)} %bitcast.92), kind=kLoop, calls=%fused_computation.19 | loop fusion | flops 6291456 | bytes 12582912 | tf_op jit(solution)/shard_map/stack | solution.py:60
  63.9 6.1 %broadcast_in_dim.9 = f32[3,1,512,2048]{3,2,1,0:T(8,128)} broadcast(f32[]{:T(128)} %constant.74.clone.1), dimensions={} | broadcast | bytes 12582916 | tf_op jit(solution)/shard_map/broadcast_in_dim | solution.py:91
  70.1 39.3 %while.14 = (s32[]{:T(128)}, f32[512,512]{1,0:T(8,128)S(1)}, f32[3,1,512,2048]{3,2,1,0:T(8,128)}, s32[]{:T(128)}, s32[3]{0:T(128)S(1)}, /*index=5*/bf16[3,1,512,...) while((s32[]{:T(128)}, f32[512,512]{1,0:T(8,128)S(1)}, ...), condition=%wide.region_1.2_spmd, body=%wide.region_0.1_spmd.sunk | while | flops 3493330944 | bytes 155194704 | solution.py:92
  74.0 6.0 %divide_convert_fusion.2 = bf16[512,512]{0,1:T(8,128)(2,1)S(1)} fusion(bf16[3,1,512,2048]{3,2,1,0:T(8,128)(2,1)} %get-tuple-element.212, s32[]{:T(128)S(6)} %select_n.46, f32[]{:T(128)} %bitcast.89, f32[]{:T(128)} %bitcast.90, f32[512]{0:T(512)S(1)} %get-tuple-element.213), kind=kOutput, calls=%fused_computation.15.clone.1 | convolution fusion | flops 1075052544 | bytes 4723716 | tf_op jit(solution)/shard_map/while/body/dot_general | solution.py:69
  80.5 1.1 copy-done.3
  81.7 1.6 fusion.53
  83.2 1.6 fusion.54
  84.9 4.5 %copy-done.2 = f32[3,1,512,2048]{3,2,1,0:T(8,128)} copy-done((f32[3,1,512,2048]{3,2,1,0:T(8,128)}, f32[3,1,512,2048]{3,2,1,0:T(8,128)S(1)}, u32[]{:S(2)}) %copy-start.2) | copy-done | bytes 12582936 | tf_op jit(solution)/shard_map/while
  93.4 6.0 %divide_convert_fusion.2 = bf16[512,512]{0,1:T(8,128)(2,1)S(1)} fusion(bf16[3,1,512,2048]{3,2,1,0:T(8,128)(2,1)} %get-tuple-element.212, s32[]{:T(128)S(6)} %select_n.46, f32[]{:T(128)} %bitcast.89, f32[]{:T(128)} %bitcast.90, f32[512]{0:T(512)S(1)} %get-tuple-element.213), kind=kOutput, calls=%fused_computation.15.clone.1 | convolution fusion | flops 1075052544 | bytes 4723716 | tf_op jit(solution)/shard_map/while/body/dot_general | solution.py:69
  99.9 1.1 copy-done.3
  101.0 1.6 fusion.53
  102.6 1.6 fusion.54
  104.2 4.5 %copy-done.2 = f32[3,1,512,2048]{3,2,1,0:T(8,128)} copy-done((f32[3,1,512,2048]{3,2,1,0:T(8,128)}, f32[3,1,512,2048]{3,2,1,0:T(8,128)S(1)}, u32[]{:S(2)}) %copy-start.2) | copy-done | bytes 12582936 | tf_op jit(solution)/shard_map/while
  109.4 8.2 %slice_bitcast_fusion.1 = (f32[1,512,2048]{2,1,0:T(8,128)}, f32[1,512,2048]{2,1,0:T(8,128)}) fusion(f32[3,1,512,2048]{3,2,1,0:T(8,128)} %get-tuple-element.109), kind=kLoop, calls=%fused_computation.24 | loop fusion | bytes 16777216 | tf_op jit(solution)/shard_map/squeeze | solution.py:95
  117.7 19.1 %collective-permute-start.4 = (f32[1,512,2048]{2,1,0:T(8,128)}, f32[1,512,2048]{2,1,0:T(8,128)}, u32[]{:S(2)}, u32[]{:S(2)}) collective-permute-start(f32[1,512,2048]{2,1,0:T(8,128)} %get-tuple-element.129), channel_id=1, source_target_pairs={{0,1},{1,0},{2,3},{3,2},{4,5},{5,4},{6,7},{7,6},{8,9},{9,8},{10,11... | collective-permute-start | bytes 12582920 | tf_op jit(solution)/shard_map/ppermute | solution.py:13
  136.8 2.0 collective-permute-start.5
  138.8 63.4 %all-reduce.3.cloned.1.call-done = f32[512,512]{1,0:T(8,128)} async-done(((f32[512,512]{1,0:T(8,128)}), f32[512,512]{1,0:T(8,128)}) %all-reduce.3.cloned.1.call-update) | async-done | bytes 1048592 | tf_op jit(solution)/shard_map/psum | solution.py:96
  202.3 54.6 %all-reduce.5.cloned.1.call-done = f32[512,512]{1,0:T(8,128)} async-done(((f32[512,512]{1,0:T(8,128)}), f32[512,512]{1,0:T(8,128)}) %all-reduce.5.cloned.1.call-update) | async-done | bytes 1048592 | tf_op jit(solution)/shard_map/psum | solution.py:97
  256.9 3.8 %fusion.24 = bf16[1,512,2048]{2,1,0:T(8,128)(2,1)} fusion(bf16[1,512,2048]{2,1,0:T(8,128)(2,1)S(1)} %copy-done.5, f32[512,512]{1,0:T(8,128)} %all-reduce.5.cloned.1.call-done), kind=kOutput, calls=%fused_computation.26 | convolution fusion | flops 1075314688 | bytes 5242880 | tf_op jit(solution)/shard_map/ab,kbp->kap/dot_general | solution.py:100
  260.7 7.1 %fusion.23 = bf16[1,512,2048]{2,1,0:T(8,128)(2,1)} fusion(f32[1,512,2048]{2,1,0:T(8,128)} %collective-permute-done.5, f32[1,512,2048]{2,1,0:T(8,128)} %collective-permute-done.4, f32[3,1,512,2048]{3,2,1,0:T(8,128)} %get-tuple-element.109), kind=kLoop, calls=%fused_computation.22 | loop fusion | flops 3145728 | bytes 14680064 | tf_op jit(solution)/shard_map/convert_element_type | solution.py:103
  (35 shorter events, 5.5 us)
Async XLA Ops:
  7.2 6.0 %copy-start = (s32[1,8,3]{1,0,2:T(1,128)S(1)}, s32[1,8,3]{1,0,2:T(1,128)}, u32[]{:S(2)}) copy-start(s32[1,8,3]{1,0,2:T(1,128)} %param.10) | copy-start | bytes 292
  7.2 195.1 %all-reduce.3.cloned.1.call-start = ((), (), s32[]{:S(2)}) async-start(), calls=%async_computation | async-start | bytes 2097152 | tf_op jit(solution)/shard_map/psum | solution.py:96
  7.2 51.1 %collective-permute-start = (bf16[1,512,2048]{2,1,0:T(8,128)(2,1)}, bf16[1,512,2048]{2,1,0:T(8,128)(2,1)S(1)}, u32[]{:S(2)}, u32[]{:S(2)}) collective-permute-start(bf16[1,512,2048]{2,1,0:T(8,128)(2,1)} %param.7), channel_id=1, source_target_pairs={{0,1},{1,0},{2,3},{3,2},{4,5},{5,4},{6,7},{7,6},{8,9},{9,8},{10,11... | collective-permute-start | bytes 6291464 | tf_op jit(solution)/shard_map/ppermute | solution.py:13
  7.8 50.5 %collective-permute-start.1 = (bf16[1,512,2048]{2,1,0:T(8,128)(2,1)}, bf16[1,512,2048]{2,1,0:T(8,128)(2,1)}, u32[]{:S(2)}, u32[]{:S(2)}) collective-permute-start(bf16[1,512,2048]{2,1,0:T(8,128)(2,1)} %param.7), channel_id=1, source_target_pairs={{0,2},{1,3},{2,0},{3,1},{4,6},{5,7},{6,4},{7,5},{8,10},{9,11},{10,... | collective-permute-start | bytes 6291464 | tf_op jit(solution)/shard_map/ppermute | solution.py:13
  10.4 46.6 %collective-permute-start.3 = (bf16[1]{0:T(256)(128)(2,1)}, bf16[1]{0:T(256)(128)(2,1)}, u32[]{:S(2)}, u32[]{:S(2)}) collective-permute-start(bf16[1]{0:T(256)(128)(2,1)} %param.8), channel_id=1, source_target_pairs={{0,2},{1,3},{2,0},{3,1},{4,6},{5,7},{6,4},{7,5},{8,10},{9,11},{10,... | collective-permute-start | bytes 14 | tf_op jit(solution)/shard_map/ppermute | solution.py:13
  10.5 46.6 %collective-permute-start.2 = (bf16[1]{0:T(256)(128)(2,1)}, bf16[1]{0:T(256)(128)(2,1)}, u32[]{:S(2)}, u32[]{:S(2)}) collective-permute-start(bf16[1]{0:T(256)(128)(2,1)} %param.8), channel_id=1, source_target_pairs={{0,1},{1,0},{2,3},{3,2},{4,5},{5,4},{6,7},{7,6},{8,9},{9,8},{10,11... | collective-permute-start | bytes 14 | tf_op jit(solution)/shard_map/ppermute | solution.py:13
  74.0 6.5 %copy-start.1 = (f32[3,1,512,2048]{3,2,1,0:T(8,128)S(1)}, f32[3,1,512,2048]{3,2,1,0:T(8,128)}, u32[]{:S(2)}) copy-start(f32[3,1,512,2048]{3,2,1,0:T(8,128)} %get-tuple-element.198) | copy-start | bytes 37748740 | tf_op jit(solution)/shard_map/while
  74.0 7.6 %copy-start.3 = (bf16[3,1,512,2048]{3,2,1,0:T(8,128)(2,1)S(1)}, bf16[3,1,512,2048]{3,2,1,0:T(8,128)(2,1)}, u32[]{:S(2)}) copy-start(bf16[3,1,512,2048]{3,2,1,0:T(8,128)(2,1)} %get-tuple-element.212) | copy-start | bytes 18874372 | tf_op jit(solution)/shard_map/while
  84.9 4.5 %copy-start.2 = (f32[3,1,512,2048]{3,2,1,0:T(8,128)}, f32[3,1,512,2048]{3,2,1,0:T(8,128)S(1)}, u32[]{:S(2)}) copy-start(f32[3,1,512,2048]{3,2,1,0:T(8,128)S(1)} %fusion.54) | copy-start | bytes 37748740 | tf_op jit(solution)/shard_map/while
  93.4 6.5 %copy-start.1 = (f32[3,1,512,2048]{3,2,1,0:T(8,128)S(1)}, f32[3,1,512,2048]{3,2,1,0:T(8,128)}, u32[]{:S(2)}) copy-start(f32[3,1,512,2048]{3,2,1,0:T(8,128)} %get-tuple-element.198) | copy-start | bytes 37748740 | tf_op jit(solution)/shard_map/while
  93.4 7.6 %copy-start.3 = (bf16[3,1,512,2048]{3,2,1,0:T(8,128)(2,1)S(1)}, bf16[3,1,512,2048]{3,2,1,0:T(8,128)(2,1)}, u32[]{:S(2)}) copy-start(bf16[3,1,512,2048]{3,2,1,0:T(8,128)(2,1)} %get-tuple-element.212) | copy-start | bytes 18874372 | tf_op jit(solution)/shard_map/while
  104.2 4.5 %copy-start.2 = (f32[3,1,512,2048]{3,2,1,0:T(8,128)}, f32[3,1,512,2048]{3,2,1,0:T(8,128)S(1)}, u32[]{:S(2)}) copy-start(f32[3,1,512,2048]{3,2,1,0:T(8,128)S(1)} %fusion.54) | copy-start | bytes 37748740 | tf_op jit(solution)/shard_map/while
  109.4 8.3 %copy-start.4 = (f32[512,512]{1,0:T(8,128)}, f32[512,512]{1,0:T(8,128)S(1)}, u32[]{:S(2)}) copy-start(f32[512,512]{1,0:T(8,128)S(1)} %get-tuple-element.110) | copy-start | bytes 3145732
  109.4 147.5 %copy-start.5 = (bf16[1,512,2048]{2,1,0:T(8,128)(2,1)S(1)}, bf16[1,512,2048]{2,1,0:T(8,128)(2,1)}, u32[]{:S(2)}) copy-start(bf16[1,512,2048]{2,1,0:T(8,128)(2,1)} %param.7) | copy-start | bytes 6291460
  117.7 143.0 %collective-permute-start.4 = (f32[1,512,2048]{2,1,0:T(8,128)}, f32[1,512,2048]{2,1,0:T(8,128)}, u32[]{:S(2)}, u32[]{:S(2)}) collective-permute-start(f32[1,512,2048]{2,1,0:T(8,128)} %get-tuple-element.129), channel_id=1, source_target_pairs={{0,1},{1,0},{2,3},{3,2},{4,5},{5,4},{6,7},{7,6},{8,9},{9,8},{10,11... | collective-permute-start | bytes 12582920 | tf_op jit(solution)/shard_map/ppermute | solution.py:13
  136.8 123.9 %collective-permute-start.5 = (f32[1,512,2048]{2,1,0:T(8,128)}, f32[1,512,2048]{2,1,0:T(8,128)}, u32[]{:S(2)}, u32[]{:S(2)}) collective-permute-start(f32[1,512,2048]{2,1,0:T(8,128)} %get-tuple-element.130), channel_id=1, source_target_pairs={{0,2},{1,3},{2,0},{3,1},{4,6},{5,7},{6,4},{7,5},{8,10},{9,11},{10,... | collective-permute-start | bytes 12582920 | tf_op jit(solution)/shard_map/ppermute | solution.py:13
  138.8 118.1 %all-reduce.5.cloned.1.call-start = ((), (), s32[]{:S(2)}) async-start(), calls=%async_computation.1 | async-start | bytes 2097152 | tf_op jit(solution)/shard_map/psum | solution.py:97
Sparse Core Ops, SparseCore 0:
  138.9 63.3 all-reduce.2
  205.3 51.5 all-reduce.4
where the time goes:
time: 275 us
  waiting for transfers between devices  162 us (59%)
  local copies, waits for them, and re-layouts  29.9 us (11%)
  starting transfers between devices  24.5 us (9%)
  matrix products  23.1 us (8%)
  between operations  14.7 us (5%)
  other arithmetic  14.5 us (5%)
  loops' own time  6.11 us (2%)
    psum x1, waiting for transfers between devices, per_device(): density = lax.psum(density, 'mem')  63.4 us
    psum x1, waiting for transfers between devices, per_device(): density = lax.psum(density, 'grp')  54.6 us
    ppermute x6, waiting for transfers between devices, partner(): return lax.ppermute(value, axis, pairs)  43.7 us
    ppermute x6, starting transfers between devices, partner(): return lax.ppermute(value, axis, pairs)  24.4 us
    dot_general x2, matrix products, pair_terms(): lax.dot_general(left_block, right_block, (((1,), (1,)), ((), ())), prefer...  12 us
    while x12, local copies, waits for them, and re-layouts  11.3 us
    squeeze x1, local copies, waits for them, and re-layouts, per_device(): gathered = gathered + partner(totals[round_idx + 1], 'mem', round_idx)  8.24 us
    convert_element_type x1, other arithmetic, per_device(): return (gathered.astype(jnp.bfloat16), lagrangian.astype(jnp.bfloat16))  7.07 us
  transfers between devices with their start and end apart: 8, of which 3 were waited for; matrix products, arithmetic and copies ran while one was open for 3% of the time, Pallas kernels for 0%

commit v1 on v0

--- a/solution.py
+++ b/solution.py
@@ -5,6 +5,12 @@
 
 OCC_DEV = 1
 ROUNDS = 2
+
+
+def _turn_rings(arr, bus_axis):
+    current_block = lax.all_gather(arr, bus_axis)
+    z = jnp.sum(current_block, axis=0)
+    return z
 
 
 def partner(value, axis, distance):
@@ -93,7 +99,7 @@
     gathered = totals[0]
     for round_idx in range(ROUNDS):
         gathered = gathered + partner(totals[round_idx + 1], "mem", round_idx)
-    density = lax.psum(density, "mem")
+    density = _turn_rings(density, "mem")
     density = lax.psum(density, "grp")
     density_scale = 1.0 / (8.0 * lax.axis_size("grp") * lax.axis_size("mem"))
     density_tile = (density * density_scale).astype(jnp.bfloat16)

time: 275 us -> 347 us (1.26)
  waiting for transfers between devices: 162 us -> 228 us
  other arithmetic: 14.5 us -> 20 us
    all_gather x0 -> x1, waiting for transfers between devices: none -> 133 us  [_turn_rings(): current_block = lax.all_gather(arr, bus_axis)]
    psum x1 -> x0, waiting for transfers between devices: 63.4 us -> none  [per_device(): density = lax.psum(density, 'mem')]
    psum x1, waiting for transfers between devices: 54.6 us -> 30.3 us  [per_device(): density = lax.psum(density, 'grp')]
    ppermute x6, waiting for transfers between devices: 43.7 us -> 63.7 us  [partner(): return lax.ppermute(value, axis, pairs)]
    reduce_sum x0 -> x1, other arithmetic: none -> 5.46 us  [_turn_rings(): z = jnp.sum(current_block, axis=0)]
  transfers between devices with their start and end apart: 8 -> 8, of which waited for: 3 -> 4; matrix products, arithmetic and copies ran while one was open for 3% -> 7% of each run, Pallas kernels for 0% -> 0%
where the time goes in v1:
time: 347 us
  waiting for transfers between devices  228 us (66%)
  local copies, waits for them, and re-layouts  30.5 us (9%)
  starting transfers between devices  24.7 us (7%)
  matrix products  23.2 us (7%)
  other arithmetic  20 us (6%)
  between operations  14.8 us (4%)
  loops' own time  6.11 us (2%)
    all_gather x1, waiting for transfers between devices, _turn_rings(): current_block = lax.all_gather(arr, bus_axis)  133 us
    ppermute x6, waiting for transfers between devices, partner(): return lax.ppermute(value, axis, pairs)  63.7 us
    psum x1, waiting for transfers between devices, per_device(): density = lax.psum(density, 'grp')  30.3 us
    ppermute x6, starting transfers between devices, partner(): return lax.ppermute(value, axis, pairs)  24.6 us
    dot_general x2, matrix products, pair_terms(): lax.dot_general(left_block, right_block, (((1,), (1,)), ((), ())), prefer...  12 us
    while x12, local copies, waits for them, and re-layouts  11.3 us
    squeeze x1, local copies, waits for them, and re-layouts, per_device(): gathered = gathered + partner(totals[round_idx + 1], 'mem', round_idx)  7.94 us
    convert_element_type x1, other arithmetic, per_device(): return (gathered.astype(jnp.bfloat16), lagrangian.astype(jnp.bfloat16))  7.1 us
  transfers between devices with their start and end apart: 8, of which 4 were waited for; matrix products, arithmetic and copies ran while one was open for 7% of the time, Pallas kernels for 0%

profile of v1, /device:TPU:0, one launch (start us, length us, event | category | flops | bytes accessed | tf_op | source)
XLA Modules:
  0.0 346.8 jit_solution(15058601513326787112)
XLA Ops:
  7.8 2.6 collective-permute-start.1
  11.9 1.2 constant_dynamic-slice_fusion.1
  13.4 43.7 %collective-permute-done.3 = bf16[1]{0:T(256)(128)(2,1)} collective-permute-done((bf16[1]{0:T(256)(128)(2,1)}, bf16[1]{0:T(256)(128)(2,1)}, u32[]{:S(2)}, u32[]{:S(2)}) %collective-permute-start.3) | collective-permute-done | bytes 34 | tf_op jit(solution)/shard_map/ppermute | solution.py:19
  57.1 1.3 maximum_convert_fusion
  58.3 5.5 %pad_maximum_fusion = bf16[3,1,512,2048]{3,2,1,0:T(8,128)(2,1)} fusion(bf16[1,1,512,2048]{3,2,1,0:T(8,128)(2,1)} %bitcast.11, bf16[1,1,512,2048]{3,2,1,0:T(8,128)(2,1)S(1)} %bitcast.95, bf16[1,1,512,2048]{3,2,1,0:T(8,128)(2,1)} %bitcast.94), kind=kLoop, calls=%fused_computation.19 | loop fusion | flops 6291456 | bytes 12582912 | tf_op jit(solution)/shard_map/stack | solution.py:66
  63.9 6.1 %broadcast_in_dim.9 = f32[3,1,512,2048]{3,2,1,0:T(8,128)} broadcast(f32[]{:T(128)} %constant.75.clone.1), dimensions={} | broadcast | bytes 12582916 | tf_op jit(solution)/shard_map/broadcast_in_dim | solution.py:97
  70.1 39.4 %while.14 = (s32[]{:T(128)}, f32[512,512]{1,0:T(8,128)S(1)}, f32[3,1,512,2048]{3,2,1,0:T(8,128)}, s32[]{:T(128)}, s32[3]{0:T(128)S(1)}, /*index=5*/bf16[3,1,512,...) while((s32[]{:T(128)}, f32[512,512]{1,0:T(8,128)S(1)}, ...), condition=%wide.region_1.2_spmd, body=%wide.region_0.1_spmd.sunk | while | flops 3493330944 | bytes 155194704 | solution.py:98
  74.0 6.0 %divide_convert_fusion.2 = bf16[512,512]{0,1:T(8,128)(2,1)S(1)} fusion(bf16[3,1,512,2048]{3,2,1,0:T(8,128)(2,1)} %get-tuple-element.212, s32[]{:T(128)S(6)} %select_n.46, f32[]{:T(128)} %bitcast.90, f32[]{:T(128)} %bitcast.91, f32[512]{0:T(512)S(1)} %get-tuple-element.213), kind=kOutput, calls=%fused_computation.15.clone.1 | convolution fusion | flops 1075052544 | bytes 4723716 | tf_op jit(solution)/shard_map/while/body/dot_general | solution.py:75
  81.7 1.6 fusion.53
  83.3 1.7 fusion.54
  84.9 4.5 %copy-done.2 = f32[3,1,512,2048]{3,2,1,0:T(8,128)} copy-done((f32[3,1,512,2048]{3,2,1,0:T(8,128)}, f32[3,1,512,2048]{3,2,1,0:T(8,128)S(1)}, u32[]{:S(2)}) %copy-start.2) | copy-done | bytes 12582936 | tf_op jit(solution)/shard_map/while
  93.4 6.0 %divide_convert_fusion.2 = bf16[512,512]{0,1:T(8,128)(2,1)S(1)} fusion(bf16[3,1,512,2048]{3,2,1,0:T(8,128)(2,1)} %get-tuple-element.212, s32[]{:T(128)S(6)} %select_n.46, f32[]{:T(128)} %bitcast.90, f32[]{:T(128)} %bitcast.91, f32[512]{0:T(512)S(1)} %get-tuple-element.213), kind=kOutput, calls=%fused_computation.15.clone.1 | convolution fusion | flops 1075052544 | bytes 4723716 | tf_op jit(solution)/shard_map/while/body/dot_general | solution.py:75
  101.1 1.6 fusion.53
  102.7 1.7 fusion.54
  104.3 4.5 %copy-done.2 = f32[3,1,512,2048]{3,2,1,0:T(8,128)} copy-done((f32[3,1,512,2048]{3,2,1,0:T(8,128)}, f32[3,1,512,2048]{3,2,1,0:T(8,128)S(1)}, u32[]{:S(2)}) %copy-start.2) | copy-done | bytes 12582936 | tf_op jit(solution)/shard_map/while
  110.6 7.9 %slice_bitcast_fusion.1 = (f32[1,512,2048]{2,1,0:T(8,128)}, f32[1,512,2048]{2,1,0:T(8,128)}) fusion(f32[3,1,512,2048]{3,2,1,0:T(8,128)} %get-tuple-element.109), kind=kLoop, calls=%fused_computation.24 | loop fusion | bytes 16777216 | tf_op jit(solution)/shard_map/squeeze | solution.py:101
  118.5 19.2 %collective-permute-start.4 = (f32[1,512,2048]{2,1,0:T(8,128)}, f32[1,512,2048]{2,1,0:T(8,128)}, u32[]{:S(2)}, u32[]{:S(2)}) collective-permute-start(f32[1,512,2048]{2,1,0:T(8,128)} %get-tuple-element.129), channel_id=1, source_target_pairs={{0,1},{1,0},{2,3},{3,2},{4,5},{5,4},{6,7},{7,6},{8,9},{9,8},{10,11... | collective-permute-start | bytes 12582920 | tf_op jit(solution)/shard_map/ppermute | solution.py:19
  137.7 2.0 collective-permute-start.5
  139.7 133.4 %all-gather.3.cloned.1.call-done = f32[4096,512]{1,0:T(8,128)} async-done(((f32[512,512]{1,0:T(8,128)}), f32[4096,512]{1,0:T(8,128)}) %all-gather.3.cloned.1.call-update) | async-done | bytes 8388624 | tf_op jit(solution)/shard_map/all_gather | solution.py:11
  273.1 5.5 %reduce_sum.9 = f32[512,512]{1,0:T(8,128)} reduce(f32[8,512,512]{2,1,0:T(8,128)} %bitcast.93, f32[]{:T(128)} %constant.75.clone.1), dimensions={0}, to_apply=%region_2.3 | reduce | flops 1835008 | bytes 9437188 | tf_op jit(solution)/shard_map/reduce_sum | solution.py:12
  278.6 20.1 %collective-permute-done.5 = f32[1,512,2048]{2,1,0:T(8,128)} collective-permute-done((f32[1,512,2048]{2,1,0:T(8,128)}, f32[1,512,2048]{2,1,0:T(8,128)}, u32[]{:S(2)}, u32[]{:S(2)}) %collective-permute-start.5) | collective-permute-done | bytes 4194336 | tf_op jit(solution)/shard_map/ppermute | solution.py:19
  298.7 7.1 %fusion.23 = bf16[1,512,2048]{2,1,0:T(8,128)(2,1)} fusion(f32[1,512,2048]{2,1,0:T(8,128)} %collective-permute-done.5, f32[1,512,2048]{2,1,0:T(8,128)} %collective-permute-done.4, f32[3,1,512,2048]{3,2,1,0:T(8,128)} %get-tuple-element.109), kind=kLoop, calls=%fused_computation.22 | loop fusion | flops 3145728 | bytes 14680064 | tf_op jit(solution)/shard_map/convert_element_type | solution.py:109
  305.8 30.3 %all-reduce.2.cloned.1.call-done = f32[512,512]{1,0:T(8,128)} async-done(((f32[512,512]{1,0:T(8,128)}), f32[512,512]{1,0:T(8,128)}) %all-reduce.2.cloned.1.call-update) | async-done | bytes 1048592 | tf_op jit(solution)/shard_map/psum | solution.py:103
  336.1 3.8 %fusion.24 = bf16[1,512,2048]{2,1,0:T(8,128)(2,1)} fusion(bf16[1,512,2048]{2,1,0:T(8,128)(2,1)S(1)} %copy-done.5, f32[512,512]{1,0:T(8,128)} %all-reduce.2.cloned.1.call-done), kind=kOutput, calls=%fused_computation.26 | convolution fusion | flops 1075314688 | bytes 5242880 | tf_op jit(solution)/shard_map/ab,kbp->kap/dot_general | solution.py:106
  (36 shorter events, 8.7 us)
Async XLA Ops:
  7.2 6.0 %copy-start = (s32[1,8,3]{1,0,2:T(1,128)S(1)}, s32[1,8,3]{1,0,2:T(1,128)}, u32[]{:S(2)}) copy-start(s32[1,8,3]{1,0,2:T(1,128)} %param.10) | copy-start | bytes 292
  7.2 265.9 %all-gather.3.cloned.1.call-start = ((), (), s32[]{:S(2)}) async-start(), calls=%async_computation.1 | async-start | bytes 9437184 | tf_op jit(solution)/shard_map/all_gather | solution.py:11
  7.2 51.1 %collective-permute-start = (bf16[1,512,2048]{2,1,0:T(8,128)(2,1)}, bf16[1,512,2048]{2,1,0:T(8,128)(2,1)S(1)}, u32[]{:S(2)}, u32[]{:S(2)}) collective-permute-start(bf16[1,512,2048]{2,1,0:T(8,128)(2,1)} %param.7), channel_id=1, source_target_pairs={{0,1},{1,0},{2,3},{3,2},{4,5},{5,4},{6,7},{7,6},{8,9},{9,8},{10,11... | collective-permute-start | bytes 6291464 | tf_op jit(solution)/shard_map/ppermute | solution.py:19
  7.8 50.5 %collective-permute-start.1 = (bf16[1,512,2048]{2,1,0:T(8,128)(2,1)}, bf16[1,512,2048]{2,1,0:T(8,128)(2,1)}, u32[]{:S(2)}, u32[]{:S(2)}) collective-permute-start(bf16[1,512,2048]{2,1,0:T(8,128)(2,1)} %param.7), channel_id=1, source_target_pairs={{0,2},{1,3},{2,0},{3,1},{4,6},{5,7},{6,4},{7,5},{8,10},{9,11},{10,... | collective-permute-start | bytes 6291464 | tf_op jit(solution)/shard_map/ppermute | solution.py:19
  10.4 46.6 %collective-permute-start.3 = (bf16[1]{0:T(256)(128)(2,1)}, bf16[1]{0:T(256)(128)(2,1)}, u32[]{:S(2)}, u32[]{:S(2)}) collective-permute-start(bf16[1]{0:T(256)(128)(2,1)} %param.8), channel_id=1, source_target_pairs={{0,2},{1,3},{2,0},{3,1},{4,6},{5,7},{6,4},{7,5},{8,10},{9,11},{10,... | collective-permute-start | bytes 14 | tf_op jit(solution)/shard_map/ppermute | solution.py:19
  10.5 46.6 %collective-permute-start.2 = (bf16[1]{0:T(256)(128)(2,1)}, bf16[1]{0:T(256)(128)(2,1)}, u32[]{:S(2)}, u32[]{:S(2)}) collective-permute-start(bf16[1]{0:T(256)(128)(2,1)} %param.8), channel_id=1, source_target_pairs={{0,1},{1,0},{2,3},{3,2},{4,5},{5,4},{6,7},{7,6},{8,9},{9,8},{10,11... | collective-permute-start | bytes 14 | tf_op jit(solution)/shard_map/ppermute | solution.py:19
  74.0 6.5 %copy-start.1 = (f32[3,1,512,2048]{3,2,1,0:T(8,128)S(1)}, f32[3,1,512,2048]{3,2,1,0:T(8,128)}, u32[]{:S(2)}) copy-start(f32[3,1,512,2048]{3,2,1,0:T(8,128)} %get-tuple-element.198) | copy-start | bytes 37748740 | tf_op jit(solution)/shard_map/while
  74.0 7.6 %copy-start.3 = (bf16[3,1,512,2048]{3,2,1,0:T(8,128)(2,1)S(1)}, bf16[3,1,512,2048]{3,2,1,0:T(8,128)(2,1)}, u32[]{:S(2)}) copy-start(bf16[3,1,512,2048]{3,2,1,0:T(8,128)(2,1)} %get-tuple-element.212) | copy-start | bytes 18874372 | tf_op jit(solution)/shard_map/while
  84.9 4.5 %copy-start.2 = (f32[3,1,512,2048]{3,2,1,0:T(8,128)}, f32[3,1,512,2048]{3,2,1,0:T(8,128)S(1)}, u32[]{:S(2)}) copy-start(f32[3,1,512,2048]{3,2,1,0:T(8,128)S(1)} %fusion.54) | copy-start | bytes 37748740 | tf_op jit(solution)/shard_map/while
  93.4 6.5 %copy-start.1 = (f32[3,1,512,2048]{3,2,1,0:T(8,128)S(1)}, f32[3,1,512,2048]{3,2,1,0:T(8,128)}, u32[]{:S(2)}) copy-start(f32[3,1,512,2048]{3,2,1,0:T(8,128)} %get-tuple-element.198) | copy-start | bytes 37748740 | tf_op jit(solution)/shard_map/while
  93.4 7.6 %copy-start.3 = (bf16[3,1,512,2048]{3,2,1,0:T(8,128)(2,1)S(1)}, bf16[3,1,512,2048]{3,2,1,0:T(8,128)(2,1)}, u32[]{:S(2)}) copy-start(bf16[3,1,512,2048]{3,2,1,0:T(8,128)(2,1)} %get-tuple-element.212) | copy-start | bytes 18874372 | tf_op jit(solution)/shard_map/while
  104.3 4.5 %copy-start.2 = (f32[3,1,512,2048]{3,2,1,0:T(8,128)}, f32[3,1,512,2048]{3,2,1,0:T(8,128)S(1)}, u32[]{:S(2)}) copy-start(f32[3,1,512,2048]{3,2,1,0:T(8,128)S(1)} %fusion.54) | copy-start | bytes 37748740 | tf_op jit(solution)/shard_map/while
  109.5 1.0 copy-start.4
  110.5 225.6 %all-reduce.2.cloned.1.call-start = ((), (), s32[]{:S(2)}) async-start(), calls=%async_computation | async-start | bytes 2097152 | tf_op jit(solution)/shard_map/psum | solution.py:103
  118.5 160.1 %collective-permute-start.4 = (f32[1,512,2048]{2,1,0:T(8,128)}, f32[1,512,2048]{2,1,0:T(8,128)}, u32[]{:S(2)}, u32[]{:S(2)}) collective-permute-start(f32[1,512,2048]{2,1,0:T(8,128)} %get-tuple-element.129), channel_id=1, source_target_pairs={{0,1},{1,0},{2,3},{3,2},{4,5},{5,4},{6,7},{7,6},{8,9},{9,8},{10,11... | collective-permute-start | bytes 12582920 | tf_op jit(solution)/shard_map/ppermute | solution.py:19
  137.7 161.0 %collective-permute-start.5 = (f32[1,512,2048]{2,1,0:T(8,128)}, f32[1,512,2048]{2,1,0:T(8,128)}, u32[]{:S(2)}, u32[]{:S(2)}) collective-permute-start(f32[1,512,2048]{2,1,0:T(8,128)} %get-tuple-element.130), channel_id=1, source_target_pairs={{0,2},{1,3},{2,0},{3,1},{4,6},{5,7},{6,4},{7,5},{8,10},{9,11},{10,... | collective-permute-start | bytes 12582920 | tf_op jit(solution)/shard_map/ppermute | solution.py:19
  278.6 57.5 %copy-start.5 = (bf16[1,512,2048]{2,1,0:T(8,128)(2,1)S(1)}, bf16[1,512,2048]{2,1,0:T(8,128)(2,1)}, u32[]{:S(2)}) copy-start(bf16[1,512,2048]{2,1,0:T(8,128)(2,1)} %param.7) | copy-start | bytes 6291460
Sparse Core Ops, SparseCore 0:
  110.6 162.4 all-gather.2
  278.7 57.3 all-reduce.1
